TPU v7x, 32 devices: a whole 2x2x4 slice. The times are simulated.
32 devices in a mesh: dp: 4 (over y, x), tensor: 8 (over z, core).
Axes of the slice: x: 2, y: 2, z: 4, core: 2. Of those that a mesh axis runs over, the one named last changes fastest.
Arguments:
- tokens: bfloat16 [96, 8192], P(('dp', 'tensor')), may hold values from -6 to 6
- weight_store: bfloat16 [2, 192, 128, 128], P(None, 'tensor', 'dp'), may hold values from -0.25 to 0.25
- block_cols: int32 [24, 8], P('tensor'), may hold values from 0 to 63, as said below
- block_count: int32 [24], P('tensor'), may hold values from 1 to 8, 108 in all
- block_home: int32 [8, 24], P('tensor'), may hold values from 0 to 23, each once within a row
- grad_hidden: bfloat16 [96, 3072], P('dp', 'tensor'), may hold values from -6 to 6
Outputs:
- hidden: bfloat16 [96, 3072], P('dp', 'tensor')
- grad_tokens: bfloat16 [96, 8192], P(('dp', 'tensor'))
- grad_weights: bfloat16 [2, 192, 128, 128], P(None, 'tensor', 'dp')
Inputs may be any that keep to these rules, and one draw needn't show every extreme that they name: `block_cols`: the 8 column blocks listed for one hidden block are all different. `block_count`: some hidden block has all 8 slots present. `block_home`: each row is a permutation of 0 to 23.
All inputs are finite; a program needn't handle non-finite values.
Results may differ from a plain program's by a relative error of at most 0.009.
Values may be sent and summed in bfloat16 or wider, within the bound.
A program may use at most 64 MiB of HBM per device.

v0:
```python
import jax
import jax.numpy as jnp
from jax import lax
from jax.sharding import PartitionSpec as P


def body(tokens, weight_store, block_cols, block_count, block_home, grad_hidden):
    rows_here = tokens.shape[0]
    model_width = tokens.shape[1]
    block_size = weight_store.shape[3]
    hidden_blocks, slot_count = block_cols.shape
    all_slots = hidden_blocks * slot_count
    col_blocks = model_width // block_size
    flat_cols = block_cols.reshape(-1)

    def select_blocks(rows):
        shaped = rows.reshape(rows.shape[0], col_blocks, block_size)
        return jnp.take(shaped, flat_cols, axis=1).reshape(
            rows.shape[0], hidden_blocks, slot_count, block_size
        )

    gathered = lax.all_gather(tokens, "tensor", axis=0, tiled=True)
    group_rows = gathered.shape[0]
    blocks = lax.all_gather(weight_store, "dp", axis=2, tiled=True)
    ordered = jnp.take(blocks, block_home[0], axis=1)
    present = (lax.iota(jnp.int32, slot_count)[None, :] < block_count[:, None]).astype(jnp.bfloat16)
    weights = (
        ordered.reshape(2, hidden_blocks, slot_count, block_size, block_size)
        * present[None, :, :, None, None]
    )
    picked = select_blocks(gathered)
    gate_pre = jnp.einsum("thkb,hkbc->thc", picked, weights[0], preferred_element_type=jnp.float32)
    up_pre = jnp.einsum("thkb,hkbc->thc", picked, weights[1], preferred_element_type=jnp.float32)
    gate_sigma = jax.nn.sigmoid(gate_pre)
    activated = gate_pre * gate_sigma
    hidden = (
        (activated * up_pre).astype(jnp.bfloat16).reshape(group_rows, hidden_blocks * block_size)
    )
    grad_in = grad_hidden.reshape(group_rows, hidden_blocks, block_size).astype(jnp.float32)
    grad_gate = (grad_in * up_pre * gate_sigma * (1.0 + gate_pre * (1.0 - gate_sigma))).astype(
        jnp.bfloat16
    )
    grad_up = (grad_in * activated).astype(jnp.bfloat16)
    back_term = jnp.einsum(
        "thc,hkbc->thkb", grad_gate, weights[0], preferred_element_type=jnp.float32
    )
    back_term = back_term + jnp.einsum(
        "thc,hkbc->thkb", grad_up, weights[1], preferred_element_type=jnp.float32
    )
    spread = jnp.zeros((rows_here * lax.axis_size("tensor"), col_blocks, block_size), jnp.float32)
    spread = spread.at[:, flat_cols].add(
        back_term.reshape(rows_here * lax.axis_size("tensor"), all_slots, block_size)
    )
    grad_tokens = lax.psum_scatter(
        spread.reshape(rows_here * lax.axis_size("tensor"), model_width),
        "tensor",
        scatter_dimension=0,
        tiled=True,
    ).astype(jnp.bfloat16)
    fetched = lax.all_gather(tokens, "tensor", axis=0, tiled=True)
    source = select_blocks(fetched)
    part_gate = jnp.einsum("thkb,thc->hkbc", source, grad_gate, preferred_element_type=jnp.float32)
    part_up = jnp.einsum("thkb,thc->hkbc", source, grad_up, preferred_element_type=jnp.float32)
    partial_value = (
        jnp.stack([part_gate, part_up]) * present.astype(jnp.float32)[None, :, :, None, None]
    )
    partial_value = partial_value.reshape(2, all_slots, block_size, block_size)
    grad_store = jnp.zeros_like(partial_value).at[:, block_home[0]].set(partial_value)
    summed = lax.psum_scatter(
        grad_store.astype(jnp.bfloat16), "dp", scatter_dimension=2, tiled=True
    )
    return (hidden, grad_tokens, summed)


def solution(mesh):
    return jax.shard_map(
        body,
        mesh=mesh,
        in_specs=(
            P(("dp", "tensor"), None),
            P(None, "tensor", "dp", None),
            P("tensor", None),
            P("tensor"),
            P("tensor", None),
            P("dp", "tensor"),
        ),
        out_specs=(P("dp", "tensor"), P(("dp", "tensor"), None), P(None, "tensor", "dp", None)),
        check_vma=False,
    )
```

profile of v0, /device:TPU:0, one launch (start us, length us, event | category | flops | bytes accessed | tf_op | source)
XLA Modules:
  0.0 103.6 jit_solution(13636348723635361189)
XLA Ops:
  7.2 0.7 all-gather.3.cloned.1.call-update
  8.0 0.8 reshape.154
  8.7 0.8 reshape.157
  9.5 0.5 broadcast.141
  10.0 1.3 %reduce.3 = s32[24]{0:T(128)S(1)} reduce(s32[1,24]{1,0:T(1,128)} %param.12, s32[]{:T(128)} %broadcast.141), dimensions={0}, to_apply=%param.12.reduce_sub_computation.3 | reduce | bytes 196 | tf_op args[4]
  11.3 0.1 squeeze.14
  11.4 0.7 fusion.15
  12.2 16.8 %all-gather = bf16[8,3,8192]{2,1,0:T(4,128)(2,1)S(1)} all-gather(bf16[1,3,8192]{2,1,0:T(4,128)(2,1)} %bitcast.101), channel_id=1, replica_groups=mesh['dp'=4,'tensor'=8] {'tensor'}, dimensions={0}, use_global_device_ids=true | all-gather | bytes 442368 | tf_op jit(solution)/shard_map/all_gather | solution.py:22
  29.0 0.5 reshape.153
  29.5 0.3 copy.22
  29.8 0.6 dynamic-slice
  31.1 0.6 gather_fusion.1
  31.7 0.1 broadcast_select_fusion
  31.8 11.6 %all-gather.3.cloned.1.call-done = bf16[2,24,128,128]{3,2,1,0:T(8,128)(2,1)} async-done(((bf16[2,24,32,128]{3,2,1,0:T(8,128)(2,1)}), bf16[2,24,128,128]{3,2,1,0:T(8,128)(2,1)}) %all-gather.3.cloned.1.call-update) | async-done | bytes 1572880 | tf_op jit(solution)/shard_map/all_gather | solution.py:24
  43.4 2.3 %gather_fusion = bf16[24,2,128,128]{3,2,1,0:T(8,128)(2,1)S(1)} fusion(bf16[2,24,128,128]{3,2,1,0:T(8,128)(2,1)} %all-gather.3.cloned.1.call-done, s32[1024]{0:T(1024)S(1)} %pad_clamp_fusion.1), kind=kCustom, calls=%fused_computation.1 | custom fusion | bytes 3145824 | tf_op jit(solution)/shard_map/jit(_take)/gather | solution.py:25
  45.7 0.1 copy.21
  45.8 0.3 select_multiply_fusion
  46.1 0.2 convolution_bitcast_fusion
  46.3 0.2 copy-done
  46.5 0.2 fusion.8
  46.8 0.5 fusion.1
  47.3 0.4 fusion.9
  47.7 0.6 copy.42
  48.3 0.4 fusion.16
  48.8 0.5 convolution_add_fusion
  49.3 2.0 %fusion = f32[24,2,128,128]{3,2,1,0:T(8,128)} fusion(f32[1,24,128,128]{3,2,0,1:T(8,128)S(1)} %bitcast.95, f32[1,24,128,128]{3,2,0,1:T(8,128)S(1)} %bitcast.94, f32[24]{0:T(128)S(1)} %reshape.162), kind=kLoop, calls=%fused_computation.5 | loop fusion | flops 1572864 | bytes 6291552 | tf_op jit(solution)/shard_map/mul | solution.py:65
  51.3 0.4 broadcast_in_dim.34
  51.7 4.7 %scatter_fusion.1 = f32[2,24,128,128]{3,2,1,0:T(8,128)S(1)} fusion(f32[2,24,128,128]{3,2,1,0:T(8,128)S(1)} %broadcast_in_dim.34, s32[24]{0:T(128)S(1)} %fusion.13, f32[24,2,128,128]{3,2,1,0:T(8,128)} %fusion), kind=kCustom, calls=%fused_computation.3 | custom fusion | bytes 9437280 | tf_op jit(solution)/shard_map/scatter | solution.py:68
  56.3 1.4 %convert_element_type.54 = bf16[2,24,128,128]{3,2,1,0:T(8,128)(2,1)} convert(f32[2,24,128,128]{3,2,1,0:T(8,128)S(1)} %scatter_fusion.1) | non-fusion elementwise | flops 786432 | bytes 4718592 | tf_op jit(solution)/shard_map/convert_element_type | solution.py:70
  57.8 1.9 %scatter_fusion = f32[24,64,128]{2,0,1:T(8,128)S(1)} fusion(f32[24,64,128]{2,0,1:T(8,128)S(1)} %broadcast_in_dim.33, s32[24]{0:T(128)S(1)} %fusion.14, f32[24,24,128]{2,1,0:T(8,128)S(1)} %bitcast.100), kind=kCustom, calls=%fused_computation.2 | custom fusion | flops 73728 | bytes 884832 | tf_op jit(solution)/shard_map/scatter-add | solution.py:51
  59.8 36.2 %all-reduce.2 = bf16[24,8192]{1,0:T(8,128)(2,1)S(1)} all-reduce(f32[24,8192]{1,0:T(8,128)S(1)} %copy_bitcast_fusion), channel_id=2, replica_groups=mesh['dp'=4,'tensor'=8] {'tensor'}, use_global_device_ids=true, to_apply=%region_1.3.clone | all-reduce | flops 196608 | bytes 1179648
  96.0 0.7 dynamic-slice_convert_fusion
  (18 shorter events, 0.3 us)
Async XLA Ops:
  7.2 22.7 %copy-start.2 = (u32[32]{0:T(128)S(1)}, u32[32]{0:T(128)}, u32[]{:S(2)}) copy-start(u32[32]{0:T(128)} %constant.41) | copy-start | bytes 388
  7.2 24.5 %copy-start.1 = (s32[1,24]{1,0:T(1,128)S(1)}, s32[1,24]{1,0:T(1,128)}, u32[]{:S(2)}) copy-start(s32[1,24]{1,0:T(1,128)} %param.12) | copy-start | bytes 292
  7.2 36.2 %all-gather.3.cloned.1.call-start = ((), (), s32[]{:S(2)}) async-start(), calls=%async_computation.1 | async-start | bytes 1966080 | tf_op jit(solution)/shard_map/all_gather | solution.py:24
  7.9 88.8 %reduce-scatter.2.cloned.1.call-start = ((), (), s32[]{:S(2)}) async-start(), calls=%async_computation.2 | async-start | bytes 1966080 | tf_op jit(solution)/shard_map/reduce_scatter | solution.py:69
  45.8 0.7 copy-start
Sparse Core Ops, SparseCore 0:
  9.8 33.5 all-gather.2
  57.9 30.9 reduce-scatter.1
where the time goes:
time: 104 us
  blocking collectives  53 us (51%)
  between operations  14.9 us (14%)
  local copies, waits for them, and re-layouts  13.2 us (13%)
  waiting for transfers between devices  12.3 us (12%)
  other arithmetic  7.79 us (7%)
  matrix products  2.36 us (2%)
    unnamed x1, blocking collectives  36.2 us
    all_gather x1, blocking collectives, body(): gathered = lax.all_gather(tokens, 'tensor', axis=0, tiled=True)  16.8 us
    all_gather x1, waiting for transfers between devices, body(): blocks = lax.all_gather(weight_store, 'dp', axis=2, tiled=True)  11.6 us
    scatter x1, local copies, waits for them, and re-layouts, body(): jnp.zeros_like(partial_value).at[:, block_home[0]].set(partial_value)  4.69 us
    gather x2, local copies, waits for them, and re-layouts, body(): ordered = jnp.take(blocks, block_home[0], axis=1)  2.36 us
  transfers between devices with their start and end apart: 2, of which 1 were waited for; matrix products, arithmetic and copies ran while one was open for 9% of the time, Pallas kernels for 0%

commit v1 on v0

--- a/solution.py
+++ b/solution.py
@@ -19,7 +19,15 @@
             rows.shape[0], hidden_blocks, slot_count, block_size
         )
 
-    gathered = lax.all_gather(tokens, "tensor", axis=0, tiled=True)
+    ways, here, step = (lax.axis_size("tensor"), lax.axis_index("tensor"), tokens.shape[0])
+    line, have = (tokens, 1)
+    while have < ways:
+        line = jnp.concatenate(
+            [line, lax.ppermute(line, "tensor", [(d, (d - have) % ways) for d in range(ways)])],
+            axis=0,
+        )
+        have = 2 * have
+    gathered = jnp.roll(line, here * step, axis=0)
     group_rows = gathered.shape[0]
     blocks = lax.all_gather(weight_store, "dp", axis=2, tiled=True)
     ordered = jnp.take(blocks, block_home[0], axis=1)

time: 104 us -> 118 us (1.13)
  waiting for transfers between devices: 12.3 us -> 19.2 us
  starting transfers between devices: 0.08 us -> 6.36 us
  blocking collectives: 53 us -> 49.7 us
  local copies, waits for them, and re-layouts: 13.2 us -> 16.1 us
    ppermute x0 -> x3, waiting for transfers between devices: none -> 18.5 us  [body(): lax.ppermute(line, 'tensor', [(d, (d - have) % ways) for d in range(ways)])]
    all_gather x1, waiting for transfers between devices: 11.6 us -> 0.02 us  [body(): blocks = lax.all_gather(weight_store, 'dp', axis=2, tiled=True)]
    ppermute x0 -> x3, starting transfers between devices: none -> 6.28 us  [body(): lax.ppermute(line, 'tensor', [(d, (d - have) % ways) for d in range(ways)])]
    concatenate x0 -> x1, local copies, waits for them, and re-layouts: none -> 2.19 us  [body(): gathered = jnp.roll(line, here * step, axis=0)]
    all_gather x1, blocking collectives: 16.8 us -> 15.1 us  [body(): fetched = lax.all_gather(tokens, 'tensor', axis=0, tiled=True)]
    unnamed x1, blocking collectives: 36.2 us -> 34.6 us
  transfers between devices with their start and end apart: 2 -> 5, of which waited for: 1 -> 2; matrix products, arithmetic and copies ran while one was open for 9% -> 11% of each run, Pallas kernels for 0% -> 0%
where the time goes in v1:
time: 118 us; the launch traced here: 117 us
  blocking collectives  49.7 us (42%)
  waiting for transfers between devices  19.2 us (16%)
  local copies, waits for them, and re-layouts  16.1 us (14%)
  between operations  14.9 us (13%)
  other arithmetic  8.67 us (7%)
  starting transfers between devices  6.36 us (5%)
  matrix products  2.36 us (2%)
    unnamed x1, blocking collectives  34.6 us
    ppermute x3, waiting for transfers between devices, body(): lax.ppermute(line, 'tensor', [(d, (d - have) % ways) for d in range(ways)])  18.5 us
    all_gather x1, blocking collectives, body(): fetched = lax.all_gather(tokens, 'tensor', axis=0, tiled=True)  15.1 us
    ppermute x3, starting transfers between devices, body(): lax.ppermute(line, 'tensor', [(d, (d - have) % ways) for d in range(ways)])  6.28 us
    scatter x1, local copies, waits for them, and re-layouts, body(): jnp.zeros_like(partial_value).at[:, block_home[0]].set(partial_value)  4.69 us
    gather x2, local copies, waits for them, and re-layouts, body(): ordered = jnp.take(blocks, block_home[0], axis=1)  2.36 us
  transfers between devices with their start and end apart: 5, of which 2 were waited for; matrix products, arithmetic and copies ran while one was open for 11% of the time, Pallas kernels for 0%

profile of v1, /device:TPU:0, one launch (start us, length us, event | category | flops | bytes accessed | tf_op | source)
XLA Modules:
  0.0 117.3 jit_solution(4478348819914803387)
XLA Ops:
  7.2 0.7 all-gather.3.cloned.1.call-update
  8.0 4.5 %collective-permute-start = (bf16[3,8192]{1,0:T(4,128)(2,1)}, bf16[3,8192]{1,0:T(4,128)(2,1)S(1)}, u32[]{:S(2)}, u32[]{:S(2)}) collective-permute-start(bf16[3,8192]{1,0:T(4,128)(2,1)} %param.8), channel_id=1, source_target_pairs={{0,7},{1,0},{2,1},{3,2},{4,3},{5,4},{6,5},{7,6},{8,15},{9,8},{10,9... | collective-permute-start | bytes 147464 | tf_op jit(solution)/shard_map/ppermute | solution.py:26
  12.5 0.8 reshape.158
  13.3 0.7 fusion.13
  13.9 0.5 broadcast.156
  14.5 1.3 %reduce.3 = s32[24]{0:T(128)S(1)} reduce(s32[1,24]{1,0:T(1,128)} %param.12, s32[]{:T(128)} %broadcast.156), dimensions={0}, to_apply=%param.12.reduce_sub_computation.3 | reduce | bytes 196 | tf_op args[4]
  15.9 15.1 %all-gather = bf16[8,3,8192]{2,1,0:T(4,128)(2,1)S(1)} all-gather(bf16[1,3,8192]{2,1,0:T(4,128)(2,1)} %bitcast.104), channel_id=1, replica_groups=mesh['dp'=4,'tensor'=8] {'tensor'}, dimensions={0}, use_global_device_ids=true | all-gather | bytes 442368 | tf_op jit(solution)/shard_map/all_gather | solution.py:68
  30.9 0.7 fusion.15
  31.7 0.8 reshape.161
  32.5 0.5 reshape.164
  33.3 0.6 dynamic-slice
  34.6 0.6 gather_fusion.2
  35.3 1.0 collective-permute-start.1
  36.3 4.8 %collective-permute-done.1 = bf16[6,8192]{1,0:T(8,128)(2,1)S(1)} collective-permute-done((bf16[6,8192]{1,0:T(8,128)(2,1)S(1)}, bf16[6,8192]{1,0:T(8,128)(2,1)S(1)}, u32[]{:S(2)}, u32[]{:S(2)}) %collective-permute-start.1) | collective-permute-done | bytes 98336 | tf_op jit(solution)/shard_map/ppermute | solution.py:26
  41.2 0.7 collective-permute-start.2
  41.9 13.7 %collective-permute-done.2 = bf16[12,8192]{1,0:T(8,128)(2,1)S(1)} collective-permute-done((bf16[12,8192]{1,0:T(8,128)(2,1)S(1)}, bf16[12,8192]{1,0:T(8,128)(2,1)S(1)}, u32[]{:S(2)}, u32[]{:S(2)}) %collective-permute-start.2) | collective-permute-done | bytes 196640 | tf_op jit(solution)/shard_map/ppermute | solution.py:26
  55.7 2.2 %concatenate.17 = bf16[48,8192]{1,0:T(8,128)(2,1)S(1)} concatenate(bf16[3,8192]{1,0:T(4,128)(2,1)S(1)} %copy-done, bf16[3,8192]{1,0:T(4,128)(2,1)S(1)} %collective-permute-done, bf16[6,8192]{1,0:T(8,128)(2,1)S(1)} %collective-permute-done.1, bf16[12,8192]{1,0:T(8,128)(2,1)S(1)} %collective-permute-done.2, bf16[3,8192]{1,0:T(4,128)(2,1)S(1)} %copy-done, ...), dimensions={0} | concatenate | bytes 1572864 | tf_op jit(solution)/shard_map/jit(_roll_dynamic)/concatenate | solution.py:30
  58.0 0.6 gather_fusion.1
  58.7 2.3 %gather_fusion = bf16[24,2,128,128]{3,2,1,0:T(8,128)(2,1)S(1)} fusion(bf16[2,24,128,128]{3,2,1,0:T(8,128)(2,1)} %all-gather.3.cloned.1.call-done, s32[1024]{0:T(1024)S(1)} %pad_clamp_fusion.1), kind=kCustom, calls=%fused_computation.2 | custom fusion | bytes 3145824 | tf_op jit(solution)/shard_map/jit(_take)/gather | solution.py:33
  61.1 0.3 select_multiply_fusion
  62.1 0.6 copy.54
  62.7 0.5 fusion.1
  63.2 0.4 fusion.9
  63.7 0.4 fusion.16
  64.1 0.5 convolution_add_fusion
  64.6 2.0 %fusion = f32[24,2,128,128]{3,2,1,0:T(8,128)} fusion(f32[1,24,128,128]{3,2,0,1:T(8,128)S(1)} %bitcast.103, f32[1,24,128,128]{3,2,0,1:T(8,128)S(1)} %bitcast.102, f32[24]{0:T(128)S(1)} %reshape.168), kind=kLoop, calls=%fused_computation.6 | loop fusion | flops 1572864 | bytes 6291552 | tf_op jit(solution)/shard_map/mul | solution.py:73
  66.6 0.4 broadcast_in_dim.34
  67.0 4.7 %scatter_fusion.1 = f32[2,24,128,128]{3,2,1,0:T(8,128)S(1)} fusion(f32[2,24,128,128]{3,2,1,0:T(8,128)S(1)} %broadcast_in_dim.34, s32[24]{0:T(128)S(1)} %fusion.13, f32[24,2,128,128]{3,2,1,0:T(8,128)} %fusion), kind=kCustom, calls=%fused_computation.4 | custom fusion | bytes 9437280 | tf_op jit(solution)/shard_map/scatter | solution.py:76
  71.7 1.4 %convert_element_type.54 = bf16[2,24,128,128]{3,2,1,0:T(8,128)(2,1)} convert(f32[2,24,128,128]{3,2,1,0:T(8,128)S(1)} %scatter_fusion.1) | non-fusion elementwise | flops 786432 | bytes 4718592 | tf_op jit(solution)/shard_map/convert_element_type | solution.py:78
  73.2 1.9 %scatter_fusion = f32[24,64,128]{2,0,1:T(8,128)S(1)} fusion(f32[24,64,128]{2,0,1:T(8,128)S(1)} %broadcast_in_dim.33, s32[24]{0:T(128)S(1)} %fusion.14, f32[24,24,128]{2,1,0:T(8,128)S(1)} %bitcast.107), kind=kCustom, calls=%fused_computation.3 | custom fusion | flops 73728 | bytes 884832 | tf_op jit(solution)/shard_map/scatter-add | solution.py:59
  75.2 34.6 %all-reduce.2 = bf16[24,8192]{1,0:T(8,128)(2,1)S(1)} all-reduce(f32[24,8192]{1,0:T(8,128)S(1)} %copy_bitcast_fusion), channel_id=2, replica_groups=mesh['dp'=4,'tensor'=8] {'tensor'}, use_global_device_ids=true, to_apply=%region_1.3.clone | all-reduce | flops 196608 | bytes 1179648
  109.8 0.7 dynamic-slice_convert_fusion
  (29 shorter events, 2.0 us)
Async XLA Ops:
  7.2 26.2 %copy-start.2 = (u32[32]{0:T(128)S(1)}, u32[32]{0:T(128)}, u32[]{:S(2)}) copy-start(u32[32]{0:T(128)} %constant.64) | copy-start | bytes 388
  7.2 28.0 %copy-start = (bf16[3,8192]{1,0:T(4,128)(2,1)S(1)}, bf16[3,8192]{1,0:T(4,128)(2,1)}, u32[]{:S(2)}) copy-start(bf16[3,8192]{1,0:T(4,128)(2,1)} %param.8) | copy-start | bytes 147460
  7.2 51.5 %all-gather.3.cloned.1.call-start = ((), (), s32[]{:S(2)}) async-start(), calls=%async_computation.1 | async-start | bytes 1966080 | tf_op jit(solution)/shard_map/all_gather | solution.py:32
  7.9 102.5 %reduce-scatter.2.cloned.1.call-start = ((), (), s32[]{:S(2)}) async-start(), calls=%async_computation.2 | async-start | bytes 1966080 | tf_op jit(solution)/shard_map/reduce_scatter | solution.py:77
  8.0 27.2 %collective-permute-start = (bf16[3,8192]{1,0:T(4,128)(2,1)}, bf16[3,8192]{1,0:T(4,128)(2,1)S(1)}, u32[]{:S(2)}, u32[]{:S(2)}) collective-permute-start(bf16[3,8192]{1,0:T(4,128)(2,1)} %param.8), channel_id=1, source_target_pairs={{0,7},{1,0},{2,1},{3,2},{4,3},{5,4},{6,5},{7,6},{8,15},{9,8},{10,9... | collective-permute-start | bytes 147464 | tf_op jit(solution)/shard_map/ppermute | solution.py:26
  35.3 5.8 %collective-permute-start.1 = (bf16[6,8192]{1,0:T(8,128)(2,1)S(1)}, bf16[6,8192]{1,0:T(8,128)(2,1)S(1)}, u32[]{:S(2)}, u32[]{:S(2)}) collective-permute-start(bf16[6,8192]{1,0:T(8,128)(2,1)S(1)} %pad_maximum_fusion.1), channel_id=1, source_target_pairs={{0,6},{1,7},{2,0},{3,1},{4,2},{5,3},{6,4},{7,5},{8,14},{9,15},{10,... | collective-permute-start | bytes 294920 | tf_op jit(solution)/shard_map/ppermute | solution.py:26
  41.2 14.4 %collective-permute-start.2 = (bf16[12,8192]{1,0:T(8,128)(2,1)S(1)}, bf16[12,8192]{1,0:T(8,128)(2,1)S(1)}, u32[]{:S(2)}, u32[]{:S(2)}) collective-permute-start(bf16[12,8192]{1,0:T(8,128)(2,1)S(1)} %pad_maximum_fusion), channel_id=1, source_target_pairs={{0,4},{1,5},{2,6},{3,7},{4,0},{5,1},{6,2},{7,3},{8,12},{9,13},{10,... | collective-permute-start | bytes 589832 | tf_op jit(solution)/shard_map/ppermute | solution.py:26
  61.1 0.7 copy-start.1
Sparse Core Ops, SparseCore 0:
  9.8 33.5 all-gather.2
  73.2 30.1 reduce-scatter.1
